TPU v7x, 256 devices: a whole 4x4x8 slice. The times are simulated.
256 devices in a mesh: gx: 16 (over z, y_lo), gy: 16 (over y_hi, x, core).
Axes of the slice: x: 4, y: 4 (y_hi: 2, y_lo: 2; y = y_hi * 2 + y_lo), z: 8, core: 2. Of those that a mesh axis runs over, the one named last changes fastest.
Arguments:
- psi: float32 [64, 128, 4096], P(None, 'gx', 'gy'), may hold values from -500 to 500
- potential: float32 [128, 4096], P('gx', 'gy'), may hold values from -2 to 0
Outputs:
- orbitals: float32 [64, 128, 4096], P(None, 'gx', 'gy')
All inputs are finite; a program needn't handle non-finite values.
Results may differ from a plain program's by a relative error of at most 0.0003.
Values sent between devices are 32-bit elements; how exact they have to be, the bound alone decides.
No kernel may reach another device: no remote copies, remote signals or barrier semaphores. Data moves between devices by JAX's collectives and lax.ppermute only.
A program may use at most 64 MiB of HBM per device.

v0:
```python
import jax
import jax.numpy as jnp
from jax import lax
from jax.sharding import PartitionSpec as P

NZ = 64
COEFS = (-205.0 / 72.0, 8.0 / 5.0, -1.0 / 5.0, 8.0 / 315.0, -1.0 / 560.0)
CENTER = 6.5
HALF_WIDTH = 5.5


def padded(array, sides, width):
    for axis, dim in sides:
        size, length = (lax.axis_size(axis), array.shape[dim])
        up = [(i, (i + 1) % size) for i in range(size)]
        down = [(j, i) for i, j in up]
        last = lax.slice_in_dim(array, length - width, length, axis=dim)
        first = lax.slice_in_dim(array, 0, width, axis=dim)
        before = lax.ppermute(last, axis, up)
        after = lax.ppermute(first, axis, down)
        array = jnp.concatenate([before, array, after], axis=dim)
    return array


def along_third(field, depth_index):
    laplace = 3.0 * COEFS[0] * field
    for distance in range(1, 5):
        forward = jnp.where(
            depth_index < NZ - distance,
            jnp.roll(field, -distance, 2),
            jnp.roll(field, NZ - distance, 2),
        )
        behind = jnp.where(
            depth_index >= distance, jnp.roll(field, distance, 2), jnp.roll(field, distance - NZ, 2)
        )
        laplace = laplace + COEFS[distance] * (forward + behind)
    return laplace


def hamiltonian(field, field_pot, depth_index):
    row_count = field.shape[1]
    lane_count = field.shape[2]
    padded_x = padded(field, (("gx", 1),), 4)
    laplace = along_third(field, depth_index)
    padded_y = padded(field, (("gy", 2),), 4 * NZ)
    for distance in range(1, 5):
        laplace = laplace + COEFS[distance] * (
            padded_x[:, 4 + distance : 4 + distance + row_count]
            + padded_x[:, 4 - distance : 4 - distance + row_count]
        )
        ahead_start = (4 + distance) * NZ
        back_start = (4 - distance) * NZ
        laplace = laplace + COEFS[distance] * (
            padded_y[:, :, ahead_start : ahead_start + lane_count]
            + padded_y[:, :, back_start : back_start + lane_count]
        )
    return -0.5 * laplace + field_pot * field


def orthonormal(matrix, ncount):
    local_gram = jnp.dot(matrix, matrix.T, precision=lax.Precision.HIGHEST) / ncount
    total_gram = lax.psum(local_gram, ("gx", "gy"))
    lower_factor = jnp.linalg.cholesky(total_gram)
    return lax.linalg.triangular_solve(lower_factor, matrix, left_side=True, lower=True)


def on_device(psi, potential):
    orbit_count = psi.shape[0]
    row_count = psi.shape[1]
    lane_count = psi.shape[2]
    field_pot = potential.reshape(1, row_count, lane_count)
    depth_index = lax.broadcasted_iota(jnp.int32, (1, 1, lane_count), 2) % NZ
    level_one = (hamiltonian(psi, field_pot, depth_index) - CENTER * psi) / HALF_WIDTH
    second = (
        2.0 * (hamiltonian(level_one, field_pot, depth_index) - CENTER * level_one) / HALF_WIDTH
        - psi
    )
    filtered = (
        2.0 * (hamiltonian(second, field_pot, depth_index) - CENTER * second) / HALF_WIDTH
        - level_one
    )
    matrix = filtered.reshape(orbit_count, row_count * lane_count)
    ncount = float(row_count * lane_count * lax.axis_size("gx") * lax.axis_size("gy"))
    first_pass = orthonormal(matrix, ncount)
    final_pass = orthonormal(first_pass, ncount)
    return final_pass.reshape(orbit_count, row_count, lane_count)


def solution(mesh):
    in_specs = (P(None, "gx", "gy"), P("gx", "gy"))
    out_specs = P(None, "gx", "gy")
    return jax.shard_map(
        on_device, mesh=mesh, in_specs=in_specs, out_specs=out_specs, check_vma=False
    )
```

profile of v0, /device:TPU:1, one launch (start us, length us, event | category | flops | bytes accessed | tf_op | source)
XLA Modules:
  0.0 262.9 jit_solution(8503108184494606311)
XLA Ops:
  0.0 2.6 collective-permute-start.3
  2.6 0.6 collective-permute-start.2
  3.2 1.3 fusion.198
  4.5 6.0 %collective-permute-start = (f32[64,4,256]{2,1,0:T(4,128)S(1)}, f32[64,4,256]{2,1,0:T(4,128)S(1)}, u32[]{:S(2)}, u32[]{:S(2)}) collective-permute-start(f32[64,4,256]{2,1,0:T(4,128)S(1)} %get-tuple-element.112), channel_id=1, source_target_pairs={{16,0},{32,16},{48,32},{64,48},{80,64},{96,80},{112,96},{128,112},... | collective-permute-start | bytes 786440 | tf_op jit(solution)/shard_map/ppermute | solution.py:20
  14.2 6.1 %collective-permute-done = f32[64,4,256]{2,1,0:T(4,128)S(1)} collective-permute-done((f32[64,4,256]{2,1,0:T(4,128)S(1)}, f32[64,4,256]{2,1,0:T(4,128)S(1)}, u32[]{:S(2)}, u32[]{:S(2)}) %collective-permute-start) | collective-permute-done | bytes 262176 | tf_op jit(solution)/shard_map/ppermute | solution.py:20
  20.4 3.0 %collective-permute-done.1 = f32[64,4,256]{2,1,0:T(4,128)S(1)} collective-permute-done((f32[64,4,256]{2,1,0:T(4,128)S(1)}, f32[64,4,256]{2,1,0:T(4,128)S(1)}, u32[]{:S(2)}, u32[]{:S(2)}) %collective-permute-start.1) | collective-permute-done | bytes 262176 | tf_op jit(solution)/shard_map/ppermute | solution.py:19
  23.4 3.3 %broadcast_multiply_fusion = (f32[64,8,256]{2,1,0:T(8,128)S(1)}, f32[64,8,256]{2,1,0:T(8,128)S(1)}) fusion(f32[64,8,256]{2,1,0:T(8,128)S(1)} %copy-done, f32[8,256]{1,0:T(8,128)S(1)} %copy-done.1, f32[64,8,256]{2,1,0:T(8,128)S(1)} %collective-permute-done.2, f32[64,8,256]{2,1,0:T(8,128)S(1)} %collective-permute-done.3, ...), kind=kLoop, calls=%fused_computation.221 | loop fusion | flops 9306112 | bytes 16525312 | tf_op jit(solution)/shard_map/div | solution.py:73
  29.2 1.5 collective-permute-start.6
  31.0 6.1 %collective-permute-start.4 = (f32[64,4,256]{2,1,0:T(4,128)S(1)}, f32[64,4,256]{2,1,0:T(4,128)S(1)}, u32[]{:S(2)}, u32[]{:S(2)}) collective-permute-start(f32[64,4,256]{2,1,0:T(4,128)S(1)} %get-tuple-element.75), channel_id=1, source_target_pairs={{16,0},{32,16},{48,32},{64,48},{80,64},{96,80},{112,96},{128,112},... | collective-permute-start | bytes 786440 | tf_op jit(solution)/shard_map/ppermute | solution.py:20
  37.5 3.5 %collective-permute-done.4 = f32[64,4,256]{2,1,0:T(4,128)S(1)} collective-permute-done((f32[64,4,256]{2,1,0:T(4,128)S(1)}, f32[64,4,256]{2,1,0:T(4,128)S(1)}, u32[]{:S(2)}, u32[]{:S(2)}) %collective-permute-start.4) | collective-permute-done | bytes 262176 | tf_op jit(solution)/shard_map/ppermute | solution.py:20
  41.0 10.6 %collective-permute-done.5 = f32[64,4,256]{2,1,0:T(4,128)S(1)} collective-permute-done((f32[64,4,256]{2,1,0:T(4,128)S(1)}, f32[64,4,256]{2,1,0:T(4,128)S(1)}, u32[]{:S(2)}, u32[]{:S(2)}) %collective-permute-start.5) | collective-permute-done | bytes 262176 | tf_op jit(solution)/shard_map/ppermute | solution.py:19
  51.6 3.7 %fusion.33 = f32[64,8,256]{2,1,0:T(8,128)S(1)} fusion(f32[64,8,256]{2,1,0:T(8,128)S(1)} %copy-done, f32[64,8,256]{2,1,0:T(8,128)S(1)} %collective-permute-done.7, f32[64,8,256]{2,1,0:T(8,128)S(1)} %get-tuple-element.6, f32[64,8,256]{2,1,0:T(8,128)S(1)} %collective-permute-done.6, f32[64,4,256]{2,1,0:T(4,128)S(1)} %collective-permute-done.5, ...), kind=kLoop, calls=%fused_computation.81 | loop fusion | flops 10747904 | bytes 12068864 | tf_op jit(solution)/shard_map/sub | solution.py:75
  56.6 1.3 collective-permute-start.10
  59.5 4.7 %collective-permute-start.8 = (f32[64,4,256]{2,1,0:T(4,128)S(1)}, f32[64,4,256]{2,1,0:T(4,128)S(1)}, u32[]{:S(2)}, u32[]{:S(2)}) collective-permute-start(f32[64,4,256]{2,1,0:T(4,128)S(1)} %get-tuple-element.41), channel_id=1, source_target_pairs={{16,0},{32,16},{48,32},{64,48},{80,64},{96,80},{112,96},{128,112},... | collective-permute-start | bytes 786440 | tf_op jit(solution)/shard_map/ppermute | solution.py:20
  64.7 3.0 %collective-permute-done.8 = f32[64,4,256]{2,1,0:T(4,128)S(1)} collective-permute-done((f32[64,4,256]{2,1,0:T(4,128)S(1)}, f32[64,4,256]{2,1,0:T(4,128)S(1)}, u32[]{:S(2)}, u32[]{:S(2)}) %collective-permute-start.8) | collective-permute-done | bytes 262176 | tf_op jit(solution)/shard_map/ppermute | solution.py:20
  67.6 12.3 %collective-permute-done.9 = f32[64,4,256]{2,1,0:T(4,128)S(1)} collective-permute-done((f32[64,4,256]{2,1,0:T(4,128)S(1)}, f32[64,4,256]{2,1,0:T(4,128)S(1)}, u32[]{:S(2)}, u32[]{:S(2)}) %collective-permute-start.9) | collective-permute-done | bytes 262176 | tf_op jit(solution)/shard_map/ppermute | solution.py:19
  80.0 3.7 %fusion.13 = f32[64,8,256]{2,1,0:T(8,128)S(1)} fusion(f32[64,8,256]{2,1,0:T(8,128)S(1)} %collective-permute-done.11, f32[64,8,256]{2,1,0:T(8,128)S(1)} %fusion.33, f32[64,8,256]{2,1,0:T(8,128)S(1)} %collective-permute-done.10, f32[64,4,256]{2,1,0:T(4,128)S(1)} %collective-permute-done.9, f32[64,4,256]{2,1,0:T(4,128)S(1)} %collective-permute-done.8, ...), kind=kLoop, calls=%fused_computation.61 | loop fusion | flops 10878976 | bytes 11544576 | tf_op jit(solution)/shard_map/sub | solution.py:79
  83.7 0.7 fusion
  84.4 78.3 %psum.14 = f32[64,64]{0,1:T(8,128)S(1)} all-reduce(f32[64,64]{0,1:T(8,128)S(1)} %fusion), channel_id=1, replica_groups=mesh['gx'=16,'gy'=16] {'gx','gy'}, use_global_device_ids=true, to_apply=%region_0.1 | all-reduce | flops 4096 | bytes 32768 | tf_op jit(solution)/shard_map/psum | solution.py:62
  162.9 5.8 %cholesky.44 = f32[64,64]{1,0:T(8,128)S(1)} custom-call(f32[64,64]{1,0:T(8,128)S(1)} %fusion.144), custom_call_target="Cholesky" | custom-call | tf_op jit(solution)/shard_map/jit(cholesky)/cholesky | solution.py:63
  168.7 0.6 compare_reduce_fusion.1
  169.4 0.7 fusion.137
  170.0 4.9 %custom-call.6 = f32[1,64,64]{1,2,0:T(8,128)S(1)} custom-call(f32[1,64,64]{2,1,0:T(8,128)S(1)} %fusion.137), custom_call_target="InvertDiagBlocksLowerTriangular" | custom-call | tf_op jit(solution)/shard_map/triangular_solve/custom-call.0 | solution.py:64
  175.1 0.6 fusion.142
  175.8 0.6 convolution_multiply_fusion
  176.3 72.7 %psum.15 = f32[64,64]{0,1:T(8,128)S(1)} all-reduce(f32[64,64]{0,1:T(8,128)S(1)} %convolution_multiply_fusion), channel_id=1, replica_groups=mesh['gx'=16,'gy'=16] {'gx','gy'}, use_global_device_ids=true, to_apply=%region_3.6 | all-reduce | flops 4096 | bytes 32768 | tf_op jit(solution)/shard_map/psum | solution.py:62
  249.2 5.8 %cholesky.55 = f32[64,64]{1,0:T(8,128)S(1)} custom-call(f32[64,64]{1,0:T(8,128)S(1)} %fusion.141), custom_call_target="Cholesky" | custom-call | tf_op jit(solution)/shard_map/jit(cholesky)/cholesky | solution.py:63
  255.0 0.6 compare_reduce_fusion
  255.7 0.7 fusion.138
  256.4 4.9 %custom-call.7 = f32[1,64,64]{1,2,0:T(8,128)S(1)} custom-call(f32[1,64,64]{2,1,0:T(8,128)S(1)} %fusion.138), custom_call_target="InvertDiagBlocksLowerTriangular" | custom-call | tf_op jit(solution)/shard_map/triangular_solve/custom-call.0 | solution.py:64
  261.2 0.6 fusion.139
  261.9 1.0 copy.13
  (81 shorter events, 10.4 us)
Async XLA Ops:
  0.0 10.6 %copy-start = (f32[64,8,256]{2,1,0:T(8,128)S(1)}, f32[64,8,256]{2,1,0:T(8,128)}, u32[]{:S(2)}) copy-start(f32[64,8,256]{2,1,0:T(8,128)} %param.5) | copy-start | bytes 1572868
  0.0 13.9 %collective-permute-start.3 = (f32[64,8,256]{2,1,0:T(8,128)}, f32[64,8,256]{2,1,0:T(8,128)S(1)}, u32[]{:S(2)}, u32[]{:S(2)}) collective-permute-start(f32[64,8,256]{2,1,0:T(8,128)} %param.5), channel_id=1, source_target_pairs={{0,1},{1,2},{2,3},{3,4},{4,5},{5,6},{6,7},{7,8},{8,9},{9,10},{10,1... | collective-permute-start | bytes 1572872 | tf_op jit(solution)/shard_map/ppermute | solution.py:19
  2.6 17.7 %collective-permute-start.2 = (f32[64,8,256]{2,1,0:T(8,128)}, f32[64,8,256]{2,1,0:T(8,128)S(1)}, u32[]{:S(2)}, u32[]{:S(2)}) collective-permute-start(f32[64,8,256]{2,1,0:T(8,128)} %param.5), channel_id=1, source_target_pairs={{1,0},{2,1},{3,2},{4,3},{5,4},{6,5},{7,6},{8,7},{9,8},{10,9},{11,1... | collective-permute-start | bytes 1572872 | tf_op jit(solution)/shard_map/ppermute | solution.py:20
  4.5 15.7 %collective-permute-start = (f32[64,4,256]{2,1,0:T(4,128)S(1)}, f32[64,4,256]{2,1,0:T(4,128)S(1)}, u32[]{:S(2)}, u32[]{:S(2)}) collective-permute-start(f32[64,4,256]{2,1,0:T(4,128)S(1)} %get-tuple-element.112), channel_id=1, source_target_pairs={{16,0},{32,16},{48,32},{64,48},{80,64},{96,80},{112,96},{128,112},... | collective-permute-start | bytes 786440 | tf_op jit(solution)/shard_map/ppermute | solution.py:20
  10.6 12.9 %collective-permute-start.1 = (f32[64,4,256]{2,1,0:T(4,128)S(1)}, f32[64,4,256]{2,1,0:T(4,128)S(1)}, u32[]{:S(2)}, u32[]{:S(2)}) collective-permute-start(f32[64,4,256]{2,1,0:T(4,128)S(1)} %get-tuple-element.113), channel_id=1, source_target_pairs={{0,16},{16,32},{32,48},{48,64},{64,80},{80,96},{96,112},{112,128},... | collective-permute-start | bytes 786440 | tf_op jit(solution)/shard_map/ppermute | solution.py:19
  13.0 0.7 copy-start.1
  29.2 22.3 %collective-permute-start.6 = (f32[64,8,256]{2,1,0:T(8,128)S(1)}, f32[64,8,256]{2,1,0:T(8,128)S(1)}, u32[]{:S(2)}, u32[]{:S(2)}) collective-permute-start(f32[64,8,256]{2,1,0:T(8,128)S(1)} %get-tuple-element.6), channel_id=1, source_target_pairs={{1,0},{2,1},{3,2},{4,3},{5,4},{6,5},{7,6},{8,7},{9,8},{10,9},{11,1... | collective-permute-start | bytes 1572872 | tf_op jit(solution)/shard_map/ppermute | solution.py:20
  30.7 20.9 %collective-permute-start.7 = (f32[64,8,256]{2,1,0:T(8,128)S(1)}, f32[64,8,256]{2,1,0:T(8,128)S(1)}, u32[]{:S(2)}, u32[]{:S(2)}) collective-permute-start(f32[64,8,256]{2,1,0:T(8,128)S(1)} %get-tuple-element.6), channel_id=1, source_target_pairs={{0,1},{1,2},{2,3},{3,4},{4,5},{5,6},{6,7},{7,8},{8,9},{9,10},{10,1... | collective-permute-start | bytes 1572872 | tf_op jit(solution)/shard_map/ppermute | solution.py:19
  31.0 10.0 %collective-permute-start.4 = (f32[64,4,256]{2,1,0:T(4,128)S(1)}, f32[64,4,256]{2,1,0:T(4,128)S(1)}, u32[]{:S(2)}, u32[]{:S(2)}) collective-permute-start(f32[64,4,256]{2,1,0:T(4,128)S(1)} %get-tuple-element.75), channel_id=1, source_target_pairs={{16,0},{32,16},{48,32},{64,48},{80,64},{96,80},{112,96},{128,112},... | collective-permute-start | bytes 786440 | tf_op jit(solution)/shard_map/ppermute | solution.py:20
  37.1 14.5 %collective-permute-start.5 = (f32[64,4,256]{2,1,0:T(4,128)S(1)}, f32[64,4,256]{2,1,0:T(4,128)S(1)}, u32[]{:S(2)}, u32[]{:S(2)}) collective-permute-start(f32[64,4,256]{2,1,0:T(4,128)S(1)} %get-tuple-element.76), channel_id=1, source_target_pairs={{0,16},{16,32},{32,48},{48,64},{64,80},{80,96},{96,112},{112,128},... | collective-permute-start | bytes 786440 | tf_op jit(solution)/shard_map/ppermute | solution.py:19
  56.6 23.4 %collective-permute-start.10 = (f32[64,8,256]{2,1,0:T(8,128)S(1)}, f32[64,8,256]{2,1,0:T(8,128)S(1)}, u32[]{:S(2)}, u32[]{:S(2)}) collective-permute-start(f32[64,8,256]{2,1,0:T(8,128)S(1)} %fusion.33), channel_id=1, source_target_pairs={{1,0},{2,1},{3,2},{4,3},{5,4},{6,5},{7,6},{8,7},{9,8},{10,9},{11,1... | collective-permute-start | bytes 1572872 | tf_op jit(solution)/shard_map/ppermute | solution.py:20
  57.9 22.1 %collective-permute-start.11 = (f32[64,8,256]{2,1,0:T(8,128)S(1)}, f32[64,8,256]{2,1,0:T(8,128)S(1)}, u32[]{:S(2)}, u32[]{:S(2)}) collective-permute-start(f32[64,8,256]{2,1,0:T(8,128)S(1)} %fusion.33), channel_id=1, source_target_pairs={{0,1},{1,2},{2,3},{3,4},{4,5},{5,6},{6,7},{7,8},{8,9},{9,10},{10,1... | collective-permute-start | bytes 1572872 | tf_op jit(solution)/shard_map/ppermute | solution.py:19
  59.5 8.1 %collective-permute-start.8 = (f32[64,4,256]{2,1,0:T(4,128)S(1)}, f32[64,4,256]{2,1,0:T(4,128)S(1)}, u32[]{:S(2)}, u32[]{:S(2)}) collective-permute-start(f32[64,4,256]{2,1,0:T(4,128)S(1)} %get-tuple-element.41), channel_id=1, source_target_pairs={{16,0},{32,16},{48,32},{64,48},{80,64},{96,80},{112,96},{128,112},... | collective-permute-start | bytes 786440 | tf_op jit(solution)/shard_map/ppermute | solution.py:20
  64.2 15.7 %collective-permute-start.9 = (f32[64,4,256]{2,1,0:T(4,128)S(1)}, f32[64,4,256]{2,1,0:T(4,128)S(1)}, u32[]{:S(2)}, u32[]{:S(2)}) collective-permute-start(f32[64,4,256]{2,1,0:T(4,128)S(1)} %get-tuple-element.42), channel_id=1, source_target_pairs={{0,16},{16,32},{32,48},{48,64},{64,80},{80,96},{96,112},{112,128},... | collective-permute-start | bytes 786440 | tf_op jit(solution)/shard_map/ppermute | solution.py:19
where the time goes:
time: 263 us
  blocking collectives  151 us (57%)
  waiting for transfers between devices  38.5 us (15%)
  other arithmetic  35 us (13%)
  starting transfers between devices  23.7 us (9%)
  local copies, waits for them, and re-layouts  11.6 us (4%)
    psum x2, blocking collectives, orthonormal(): total_gram = lax.psum(local_gram, ('gx', 'gy'))  151 us
    ppermute x6, waiting for transfers between devices, padded(): before = lax.ppermute(last, axis, up)  25.9 us
    ppermute x6, starting transfers between devices, padded(): after = lax.ppermute(first, axis, down)  20.2 us
    another operation x6, other arithmetic, orthonormal(): lower_factor = jnp.linalg.cholesky(total_gram)  13 us
    ppermute x6, waiting for transfers between devices, padded(): after = lax.ppermute(first, axis, down)  12.5 us
    another operation x4, other arithmetic, orthonormal(): lax.linalg.triangular_solve(lower_factor, matrix, left_side=True, lower=T...  11.1 us
  transfers between devices with their start and end apart: 12, of which 6 were waited for; matrix products, arithmetic and copies ran while one was open for 2% of the time, Pallas kernels for 0%

commit v1 on v0

--- a/solution.py
+++ b/solution.py
@@ -59,7 +59,7 @@
 
 def orthonormal(matrix, ncount):
     local_gram = jnp.dot(matrix, matrix.T, precision=lax.Precision.HIGHEST) / ncount
-    total_gram = lax.psum(local_gram, ("gx", "gy"))
+    total_gram = lax.psum(lax.psum(local_gram, "gy"), "gx")
     lower_factor = jnp.linalg.cholesky(total_gram)
     return lax.linalg.triangular_solve(lower_factor, matrix, left_side=True, lower=True)
 

time: 263 us -> 369 us (1.40)
  the two profiles are of different devices: /device:TPU:1 before, /device:TPU:16 now
where the time goes in v1:
time: 369 us; the launch traced here: 368 us
  blocking collectives  258 us (70%)
  other arithmetic  35.3 us (10%)
  starting transfers between devices  32.2 us (9%)
  waiting for transfers between devices  27.8 us (8%)
  local copies, waits for them, and re-layouts  11.6 us (3%)
    psum x4, blocking collectives, orthonormal(): total_gram = lax.psum(lax.psum(local_gram, 'gy'), 'gx')  258 us
    ppermute x6, starting transfers between devices, padded(): after = lax.ppermute(first, axis, down)  32.2 us
    ppermute x6, waiting for transfers between devices, padded(): after = lax.ppermute(first, axis, down)  27.8 us
    another operation x6, other arithmetic, orthonormal(): lower_factor = jnp.linalg.cholesky(total_gram)  13 us
    another operation x4, other arithmetic, orthonormal(): lax.linalg.triangular_solve(lower_factor, matrix, left_side=True, lower=T...  11.1 us
  transfers between devices with their start and end apart: 12, of which 3 were waited for; matrix products, arithmetic and copies ran while one was open for 2% of the time, Pallas kernels for 0%

profile of v1, /device:TPU:16, one launch (start us, length us, event | category | flops | bytes accessed | tf_op | source)
XLA Modules:
  0.0 368.4 jit_solution(14094657103007111270)
XLA Ops:
  0.0 5.4 %collective-permute-start.2 = (f32[64,8,256]{2,1,0:T(8,128)}, f32[64,8,256]{2,1,0:T(8,128)S(1)}, u32[]{:S(2)}, u32[]{:S(2)}) collective-permute-start(f32[64,8,256]{2,1,0:T(8,128)} %param.5), channel_id=1, source_target_pairs={{1,0},{2,1},{3,2},{4,3},{5,4},{6,5},{7,6},{8,7},{9,8},{10,9},{11,1... | collective-permute-start | bytes 1572872 | tf_op jit(solution)/shard_map/ppermute | solution.py:20
  5.4 1.3 fusion.198
  6.7 6.7 %collective-permute-start = (f32[64,4,256]{2,1,0:T(4,128)S(1)}, f32[64,4,256]{2,1,0:T(4,128)S(1)}, u32[]{:S(2)}, u32[]{:S(2)}) collective-permute-start(f32[64,4,256]{2,1,0:T(4,128)S(1)} %get-tuple-element.112), channel_id=1, source_target_pairs={{16,0},{32,16},{48,32},{64,48},{80,64},{96,80},{112,96},{128,112},... | collective-permute-start | bytes 786440 | tf_op jit(solution)/shard_map/ppermute | solution.py:20
  13.5 0.2 fusion.194
  15.9 0.6 copy-done.1
  16.9 5.5 %collective-permute-done = f32[64,4,256]{2,1,0:T(4,128)S(1)} collective-permute-done((f32[64,4,256]{2,1,0:T(4,128)S(1)}, f32[64,4,256]{2,1,0:T(4,128)S(1)}, u32[]{:S(2)}, u32[]{:S(2)}) %collective-permute-start) | collective-permute-done | bytes 262176 | tf_op jit(solution)/shard_map/ppermute | solution.py:20
  22.6 3.4 broadcast_multiply_fusion
  28.5 3.1 collective-permute-start.6
  31.6 7.7 %collective-permute-start.4 = (f32[64,4,256]{2,1,0:T(4,128)S(1)}, f32[64,4,256]{2,1,0:T(4,128)S(1)}, u32[]{:S(2)}, u32[]{:S(2)}) collective-permute-start(f32[64,4,256]{2,1,0:T(4,128)S(1)} %get-tuple-element.75), channel_id=1, source_target_pairs={{16,0},{32,16},{48,32},{64,48},{80,64},{96,80},{112,96},{128,112},... | collective-permute-start | bytes 786440 | tf_op jit(solution)/shard_map/ppermute | solution.py:20
  39.7 10.2 %collective-permute-done.4 = f32[64,4,256]{2,1,0:T(4,128)S(1)} collective-permute-done((f32[64,4,256]{2,1,0:T(4,128)S(1)}, f32[64,4,256]{2,1,0:T(4,128)S(1)}, u32[]{:S(2)}, u32[]{:S(2)}) %collective-permute-start.4) | collective-permute-done | bytes 262176 | tf_op jit(solution)/shard_map/ppermute | solution.py:20
  49.9 3.8 %fusion.33 = f32[64,8,256]{2,1,0:T(8,128)S(1)} fusion(f32[64,8,256]{2,1,0:T(8,128)S(1)} %copy-done, f32[64,8,256]{2,1,0:T(8,128)S(1)} %collective-permute-done.7, f32[64,8,256]{2,1,0:T(8,128)S(1)} %get-tuple-element.6, f32[64,8,256]{2,1,0:T(8,128)S(1)} %collective-permute-done.6, f32[64,4,256]{2,1,0:T(4,128)S(1)} %collective-permute-done.5, ...), kind=kLoop, calls=%fused_computation.81 | loop fusion | flops 10747904 | bytes 12068864 | tf_op jit(solution)/shard_map/sub | solution.py:75
  55.1 3.2 collective-permute-start.10
  59.4 6.1 %collective-permute-start.8 = (f32[64,4,256]{2,1,0:T(4,128)S(1)}, f32[64,4,256]{2,1,0:T(4,128)S(1)}, u32[]{:S(2)}, u32[]{:S(2)}) collective-permute-start(f32[64,4,256]{2,1,0:T(4,128)S(1)} %get-tuple-element.41), channel_id=1, source_target_pairs={{16,0},{32,16},{48,32},{64,48},{80,64},{96,80},{112,96},{128,112},... | collective-permute-start | bytes 786440 | tf_op jit(solution)/shard_map/ppermute | solution.py:20
  66.0 12.0 %collective-permute-done.8 = f32[64,4,256]{2,1,0:T(4,128)S(1)} collective-permute-done((f32[64,4,256]{2,1,0:T(4,128)S(1)}, f32[64,4,256]{2,1,0:T(4,128)S(1)}, u32[]{:S(2)}, u32[]{:S(2)}) %collective-permute-start.8) | collective-permute-done | bytes 262176 | tf_op jit(solution)/shard_map/ppermute | solution.py:20
  78.0 3.8 %fusion.13 = f32[64,8,256]{2,1,0:T(8,128)S(1)} fusion(f32[64,8,256]{2,1,0:T(8,128)S(1)} %collective-permute-done.11, f32[64,8,256]{2,1,0:T(8,128)S(1)} %fusion.33, f32[64,8,256]{2,1,0:T(8,128)S(1)} %collective-permute-done.10, f32[64,4,256]{2,1,0:T(4,128)S(1)} %collective-permute-done.9, f32[64,4,256]{2,1,0:T(4,128)S(1)} %collective-permute-done.8, ...), kind=kLoop, calls=%fused_computation.61 | loop fusion | flops 10878976 | bytes 11544576 | tf_op jit(solution)/shard_map/sub | solution.py:79
  81.9 0.7 fusion
  82.6 67.3 %psum.28 = f32[64,64]{0,1:T(8,128)S(1)} all-reduce(f32[64,64]{0,1:T(8,128)S(1)} %fusion), channel_id=1, replica_groups=mesh['gx'=16,'gy'=16] {'gy'}, use_global_device_ids=true, to_apply=%region_0.1 | all-reduce | flops 4096 | bytes 32768 | tf_op jit(solution)/shard_map/psum | solution.py:62
  149.9 66.3 %psum.29 = f32[64,64]{0,1:T(8,128)S(1)} all-reduce(f32[64,64]{0,1:T(8,128)S(1)} %psum.28), channel_id=1, replica_groups=mesh['gx'=16,'gy'=16] {'gx'}, use_global_device_ids=true, to_apply=%region_1.2 | all-reduce | flops 4096 | bytes 32768 | tf_op jit(solution)/shard_map/psum | solution.py:62
  216.3 5.8 %cholesky.44 = f32[64,64]{1,0:T(8,128)S(1)} custom-call(f32[64,64]{1,0:T(8,128)S(1)} %fusion.144), custom_call_target="Cholesky" | custom-call | tf_op jit(solution)/shard_map/jit(cholesky)/cholesky | solution.py:63
  222.2 0.6 compare_reduce_fusion.1
  222.8 0.7 fusion.137
  223.5 4.9 %custom-call.6 = f32[1,64,64]{1,2,0:T(8,128)S(1)} custom-call(f32[1,64,64]{2,1,0:T(8,128)S(1)} %fusion.137), custom_call_target="InvertDiagBlocksLowerTriangular" | custom-call | tf_op jit(solution)/shard_map/triangular_solve/custom-call.0 | solution.py:64
  228.6 0.6 fusion.142
  229.2 0.6 convolution_multiply_fusion
  229.8 65.0 %psum.30 = f32[64,64]{0,1:T(8,128)S(1)} all-reduce(f32[64,64]{0,1:T(8,128)S(1)} %convolution_multiply_fusion), channel_id=1, replica_groups=mesh['gx'=16,'gy'=16] {'gy'}, use_global_device_ids=true, to_apply=%region_4.7 | all-reduce | flops 4096 | bytes 32768 | tf_op jit(solution)/shard_map/psum | solution.py:62
  294.7 59.8 %psum.31 = f32[64,64]{0,1:T(8,128)S(1)} all-reduce(f32[64,64]{0,1:T(8,128)S(1)} %psum.30), channel_id=1, replica_groups=mesh['gx'=16,'gy'=16] {'gx'}, use_global_device_ids=true, to_apply=%region_5.8 | all-reduce | flops 4096 | bytes 32768 | tf_op jit(solution)/shard_map/psum | solution.py:62
  354.7 5.8 %cholesky.55 = f32[64,64]{1,0:T(8,128)S(1)} custom-call(f32[64,64]{1,0:T(8,128)S(1)} %fusion.141), custom_call_target="Cholesky" | custom-call | tf_op jit(solution)/shard_map/jit(cholesky)/cholesky | solution.py:63
  360.6 0.6 compare_reduce_fusion
  361.2 0.7 fusion.138
  361.9 4.9 %custom-call.7 = f32[1,64,64]{1,2,0:T(8,128)S(1)} custom-call(f32[1,64,64]{2,1,0:T(8,128)S(1)} %fusion.138), custom_call_target="InvertDiagBlocksLowerTriangular" | custom-call | tf_op jit(solution)/shard_map/triangular_solve/custom-call.0 | solution.py:64
  366.8 0.6 fusion.139
  367.4 1.0 copy.13
  (83 shorter events, 8.8 us)
Async XLA Ops:
  0.0 13.3 %copy-start = (f32[64,8,256]{2,1,0:T(8,128)S(1)}, f32[64,8,256]{2,1,0:T(8,128)}, u32[]{:S(2)}) copy-start(f32[64,8,256]{2,1,0:T(8,128)} %param.5) | copy-start | bytes 1572868
  0.0 16.7 %collective-permute-start.3 = (f32[64,8,256]{2,1,0:T(8,128)}, f32[64,8,256]{2,1,0:T(8,128)S(1)}, u32[]{:S(2)}, u32[]{:S(2)}) collective-permute-start(f32[64,8,256]{2,1,0:T(8,128)} %param.5), channel_id=1, source_target_pairs={{0,1},{1,2},{2,3},{3,4},{4,5},{5,6},{6,7},{7,8},{8,9},{9,10},{10,1... | collective-permute-start | bytes 1572872 | tf_op jit(solution)/shard_map/ppermute | solution.py:19
  0.0 22.5 %collective-permute-start.2 = (f32[64,8,256]{2,1,0:T(8,128)}, f32[64,8,256]{2,1,0:T(8,128)S(1)}, u32[]{:S(2)}, u32[]{:S(2)}) collective-permute-start(f32[64,8,256]{2,1,0:T(8,128)} %param.5), channel_id=1, source_target_pairs={{1,0},{2,1},{3,2},{4,3},{5,4},{6,5},{7,6},{8,7},{9,8},{10,9},{11,1... | collective-permute-start | bytes 1572872 | tf_op jit(solution)/shard_map/ppermute | solution.py:20
  6.7 15.8 %collective-permute-start = (f32[64,4,256]{2,1,0:T(4,128)S(1)}, f32[64,4,256]{2,1,0:T(4,128)S(1)}, u32[]{:S(2)}, u32[]{:S(2)}) collective-permute-start(f32[64,4,256]{2,1,0:T(4,128)S(1)} %get-tuple-element.112), channel_id=1, source_target_pairs={{16,0},{32,16},{48,32},{64,48},{80,64},{96,80},{112,96},{128,112},... | collective-permute-start | bytes 786440 | tf_op jit(solution)/shard_map/ppermute | solution.py:20
  13.3 9.3 %collective-permute-start.1 = (f32[64,4,256]{2,1,0:T(4,128)S(1)}, f32[64,4,256]{2,1,0:T(4,128)S(1)}, u32[]{:S(2)}, u32[]{:S(2)}) collective-permute-start(f32[64,4,256]{2,1,0:T(4,128)S(1)} %get-tuple-element.113), channel_id=1, source_target_pairs={{0,16},{16,32},{32,48},{48,64},{64,80},{80,96},{96,112},{112,128},... | collective-permute-start | bytes 786440 | tf_op jit(solution)/shard_map/ppermute | solution.py:19
  15.7 0.7 copy-start.1
  28.5 21.5 %collective-permute-start.6 = (f32[64,8,256]{2,1,0:T(8,128)S(1)}, f32[64,8,256]{2,1,0:T(8,128)S(1)}, u32[]{:S(2)}, u32[]{:S(2)}) collective-permute-start(f32[64,8,256]{2,1,0:T(8,128)S(1)} %get-tuple-element.6), channel_id=1, source_target_pairs={{1,0},{2,1},{3,2},{4,3},{5,4},{6,5},{7,6},{8,7},{9,8},{10,9},{11,1... | collective-permute-start | bytes 1572872 | tf_op jit(solution)/shard_map/ppermute | solution.py:20
  31.6 18.3 %collective-permute-start.7 = (f32[64,8,256]{2,1,0:T(8,128)S(1)}, f32[64,8,256]{2,1,0:T(8,128)S(1)}, u32[]{:S(2)}, u32[]{:S(2)}) collective-permute-start(f32[64,8,256]{2,1,0:T(8,128)S(1)} %get-tuple-element.6), channel_id=1, source_target_pairs={{0,1},{1,2},{2,3},{3,4},{4,5},{5,6},{6,7},{7,8},{8,9},{9,10},{10,1... | collective-permute-start | bytes 1572872 | tf_op jit(solution)/shard_map/ppermute | solution.py:19
  31.6 18.3 %collective-permute-start.4 = (f32[64,4,256]{2,1,0:T(4,128)S(1)}, f32[64,4,256]{2,1,0:T(4,128)S(1)}, u32[]{:S(2)}, u32[]{:S(2)}) collective-permute-start(f32[64,4,256]{2,1,0:T(4,128)S(1)} %get-tuple-element.75), channel_id=1, source_target_pairs={{16,0},{32,16},{48,32},{64,48},{80,64},{96,80},{112,96},{128,112},... | collective-permute-start | bytes 786440 | tf_op jit(solution)/shard_map/ppermute | solution.py:20
  39.3 10.6 %collective-permute-start.5 = (f32[64,4,256]{2,1,0:T(4,128)S(1)}, f32[64,4,256]{2,1,0:T(4,128)S(1)}, u32[]{:S(2)}, u32[]{:S(2)}) collective-permute-start(f32[64,4,256]{2,1,0:T(4,128)S(1)} %get-tuple-element.76), channel_id=1, source_target_pairs={{0,16},{16,32},{32,48},{48,64},{64,80},{80,96},{96,112},{112,128},... | collective-permute-start | bytes 786440 | tf_op jit(solution)/shard_map/ppermute | solution.py:19
  55.1 22.9 %collective-permute-start.10 = (f32[64,8,256]{2,1,0:T(8,128)S(1)}, f32[64,8,256]{2,1,0:T(8,128)S(1)}, u32[]{:S(2)}, u32[]{:S(2)}) collective-permute-start(f32[64,8,256]{2,1,0:T(8,128)S(1)} %fusion.33), channel_id=1, source_target_pairs={{1,0},{2,1},{3,2},{4,3},{5,4},{6,5},{7,6},{8,7},{9,8},{10,9},{11,1... | collective-permute-start | bytes 1572872 | tf_op jit(solution)/shard_map/ppermute | solution.py:20
  58.3 19.7 %collective-permute-start.11 = (f32[64,8,256]{2,1,0:T(8,128)S(1)}, f32[64,8,256]{2,1,0:T(8,128)S(1)}, u32[]{:S(2)}, u32[]{:S(2)}) collective-permute-start(f32[64,8,256]{2,1,0:T(8,128)S(1)} %fusion.33), channel_id=1, source_target_pairs={{0,1},{1,2},{2,3},{3,4},{4,5},{5,6},{6,7},{7,8},{8,9},{9,10},{10,1... | collective-permute-start | bytes 1572872 | tf_op jit(solution)/shard_map/ppermute | solution.py:19
  59.4 18.6 %collective-permute-start.8 = (f32[64,4,256]{2,1,0:T(4,128)S(1)}, f32[64,4,256]{2,1,0:T(4,128)S(1)}, u32[]{:S(2)}, u32[]{:S(2)}) collective-permute-start(f32[64,4,256]{2,1,0:T(4,128)S(1)} %get-tuple-element.41), channel_id=1, source_target_pairs={{16,0},{32,16},{48,32},{64,48},{80,64},{96,80},{112,96},{128,112},... | collective-permute-start | bytes 786440 | tf_op jit(solution)/shard_map/ppermute | solution.py:20
  65.6 12.5 %collective-permute-start.9 = (f32[64,4,256]{2,1,0:T(4,128)S(1)}, f32[64,4,256]{2,1,0:T(4,128)S(1)}, u32[]{:S(2)}, u32[]{:S(2)}) collective-permute-start(f32[64,4,256]{2,1,0:T(4,128)S(1)} %get-tuple-element.42), channel_id=1, source_target_pairs={{0,16},{16,32},{32,48},{48,64},{64,80},{80,96},{96,112},{112,128},... | collective-permute-start | bytes 786440 | tf_op jit(solution)/shard_map/ppermute | solution.py:19
